TPU v7x, 256 devices: a whole 4x4x8 slice. The times are simulated.
256 devices in a mesh: inner: 32 (over z, y_hi, core), outer: 8 (over y_lo, x).
Axes of the slice: x: 4, y: 4 (y_hi: 2, y_lo: 2; y = y_hi * 2 + y_lo), z: 8, core: 2. Of those that a mesh axis runs over, the one named last changes fastest.
Arguments:
- queries: bfloat16 [32768, 1024], P(('outer', 'inner')), may hold values from -8 to 8
- key_rows: bfloat16 [32768, 128], P(('outer', 'inner')), may hold values from -8 to 8
- value_rows: bfloat16 [32768, 128], P(('outer', 'inner')), may hold values from -6 to 6
- grad_output: bfloat16 [32768, 1024], P(('outer', 'inner')), may hold values from -6 to 6
- doc_blocks: int32 [256], replicated, may hold values from 0 to 31, never falling along the last dimension, each value on 1 to 32 neighbouring positions
Outputs:
- grad_queries: bfloat16 [32768, 1024], P(('outer', 'inner'))
- grad_keys: bfloat16 [32768, 128], P(('outer', 'inner'))
- grad_values: bfloat16 [32768, 128], P(('outer', 'inner'))
All inputs are finite; a program needn't handle non-finite values.
Results may differ from a plain program's by a relative error of at most 0.019.
Values may be sent and summed in bfloat16 or wider, within the bound.
A program may use at most 64 MiB of HBM per device.

v0:
```python
import jax
import jax.numpy as jnp
from jax import lax
from jax.sharding import PartitionSpec as P


def shifted(block, axis, distance):
    devices = range(lax.axis_size(axis))
    route = [(i - distance, i) for i in devices if i - distance in devices]
    return lax.ppermute(block, axis, route)


def shards(queries, key_rows, value_rows, grad_output, doc_blocks):
    token_count = queries.shape[0]
    width = key_rows.shape[1]
    head_count = queries.shape[1] // width
    inner_count = lax.axis_size("inner")
    outer_count = lax.axis_size("outer")
    inner_at = lax.axis_index("inner")
    outer_at = lax.axis_index("outer")
    blocks_dev = doc_blocks.shape[0] // (inner_count * outer_count)
    block_len = token_count // blocks_dev
    tile_blocks = 4
    span_blocks = inner_count * blocks_dev
    win_blocks = -(-(span_blocks + blocks_dev) // tile_blocks) * tile_blocks
    pad_blocks = max(0, (inner_count - 1) * blocks_dev + win_blocks - 2 * span_blocks)
    tile_count = win_blocks // tile_blocks
    tile_len = tile_blocks * block_len
    scaling = width ** (-0.5)
    earlier_k, earlier_v = shifted((key_rows, value_rows), "outer", 1)
    group_k, group_v, prior_k, prior_v = (
        lax.all_gather(key_rows, "inner", axis=0, tiled=True),
        lax.all_gather(value_rows, "inner", axis=0, tiled=True),
        lax.all_gather(earlier_k, "inner", axis=0, tiled=True),
        lax.all_gather(earlier_v, "inner", axis=0, tiled=True),
    )
    padding = jnp.zeros((pad_blocks * block_len, width), key_rows.dtype)
    keys_all = jnp.concatenate([prior_k, group_k, padding], axis=0)
    values_all = jnp.concatenate([prior_v, group_v, padding], axis=0)
    first_block = inner_at * blocks_dev
    key_win = lax.dynamic_slice_in_dim(keys_all, first_block * block_len, win_blocks * block_len, 0)
    value_win = lax.dynamic_slice_in_dim(
        values_all, first_block * block_len, win_blocks * block_len, 0
    )
    tags_pad = jnp.concatenate(
        [
            jnp.full((span_blocks,), -1, jnp.int32),
            doc_blocks,
            jnp.full((span_blocks + pad_blocks,), -1, jnp.int32),
        ]
    )
    key_tags = lax.dynamic_slice_in_dim(
        tags_pad, outer_at * span_blocks + first_block, win_blocks, 0
    )
    own_tags = lax.dynamic_slice_in_dim(
        doc_blocks, (outer_at * inner_count + inner_at) * blocks_dev, blocks_dev, 0
    )
    row_tags = jnp.repeat(jnp.repeat(own_tags, block_len), head_count)
    row_pos = (
        jnp.repeat(jnp.arange(token_count, dtype=jnp.int32), head_count) + span_blocks * block_len
    )
    key_tiles = key_win.reshape(tile_count, tile_len, width)
    value_tiles = value_win.reshape(tile_count, tile_len, width)
    tag_tiles = jnp.repeat(key_tags, block_len).reshape(tile_count, tile_len)
    pos_tiles = jnp.arange(win_blocks * block_len, dtype=jnp.int32).reshape(tile_count, tile_len)
    query_flat = queries.reshape(token_count * head_count, width)
    grad_flat = grad_output.reshape(token_count * head_count, width)
    row_total = token_count * head_count

    def allowed_of(tag_tile, pos_tile):
        return (row_tags[:, None] == tag_tile[None, :]) & (pos_tile[None, :] <= row_pos[:, None])

    def forward_tile(running, pieces):
        key_tile, value_tile, tag_tile, pos_tile = pieces
        allowed = allowed_of(tag_tile, pos_tile)
        row_max, row_sum, out_acc = running
        scores = (
            jnp.einsum("rd,kd->rk", query_flat, key_tile, preferred_element_type=jnp.float32)
            * scaling
        )
        masked = jnp.where(allowed, scores, -jnp.inf)
        new_max = jnp.maximum(row_max, jnp.max(masked, axis=1, keepdims=True))
        factor = jnp.exp(row_max - new_max)
        weights = jnp.exp(masked - new_max)
        new_sum = row_sum * factor + jnp.sum(weights, axis=1, keepdims=True)
        weights_high = weights.astype(jnp.bfloat16)
        weights_rest = (weights - weights_high.astype(jnp.float32)).astype(jnp.bfloat16)
        product = jnp.dot(weights_high, value_tile, preferred_element_type=jnp.float32)
        product = product + jnp.dot(weights_rest, value_tile, preferred_element_type=jnp.float32)
        new_out = out_acc * factor + product
        return ((new_max, new_sum, new_out), None)

    start_state = (
        jnp.full((row_total, 1), -1e30, jnp.float32),
        jnp.zeros((row_total, 1), jnp.float32),
        jnp.zeros((row_total, width), jnp.float32),
    )
    (row_max, row_sum, out_acc), unused_ys = lax.scan(
        forward_tile, start_state, (key_tiles, value_tiles, tag_tiles, pos_tiles)
    )
    attn_out = out_acc / row_sum
    delta = jnp.sum(grad_flat.astype(jnp.float32) * attn_out, axis=1, keepdims=True)

    def backward_tile(grad_q, pieces):
        key_tile, value_tile, tag_tile, pos_tile = pieces
        allowed = allowed_of(tag_tile, pos_tile)
        scores = (
            jnp.einsum("rd,kd->rk", query_flat, key_tile, preferred_element_type=jnp.float32)
            * scaling
        )
        probs = jnp.exp(jnp.where(allowed, scores - row_max, -jnp.inf)) / row_sum
        probs_low = probs.astype(jnp.bfloat16)
        value_part = jnp.einsum(
            "rk,rd->kd", probs_low, grad_flat, preferred_element_type=jnp.float32
        )
        dprobs = jnp.einsum("rd,kd->rk", grad_flat, value_tile, preferred_element_type=jnp.float32)
        dscores = (probs * (dprobs - delta) * scaling).astype(jnp.bfloat16)
        new_q = grad_q + jnp.dot(dscores, key_tile, preferred_element_type=jnp.float32)
        key_part = jnp.einsum("rk,rd->kd", dscores, query_flat, preferred_element_type=jnp.float32)
        return (new_q, (key_part, value_part))

    grad_q, (key_parts, value_parts) = lax.scan(
        backward_tile,
        jnp.zeros((row_total, width), jnp.float32),
        (key_tiles, value_tiles, tag_tiles, pos_tiles),
    )
    grads_win = jnp.concatenate(
        [
            key_parts.reshape(win_blocks * block_len, width),
            value_parts.reshape(win_blocks * block_len, width),
        ],
        axis=1,
    )
    canvas = jnp.zeros(((2 * span_blocks + pad_blocks) * block_len, 2 * width), jnp.float32)
    canvas = lax.dynamic_update_slice_in_dim(canvas, grads_win, first_block * block_len, 0)
    earlier_part = canvas[: span_blocks * block_len]
    group_part = canvas[span_blocks * block_len : 2 * span_blocks * block_len]
    combined = jnp.concatenate([group_part, earlier_part], axis=1)
    summed = lax.psum_scatter(
        combined.astype(jnp.bfloat16), "inner", scatter_dimension=0, tiled=True
    ).astype(jnp.float32)
    returned = shifted(summed[:, 2 * width :].astype(jnp.bfloat16), "outer", -1).astype(jnp.float32)
    grads_kv = summed[:, : 2 * width] + returned
    grad_queries = grad_q.reshape(token_count, head_count * width).astype(jnp.bfloat16)
    return (
        grad_queries,
        grads_kv[:, :width].astype(jnp.bfloat16),
        grads_kv[:, width:].astype(jnp.bfloat16),
    )


def solution(mesh):
    in_specs = (
        P(("outer", "inner"), None),
        P(("outer", "inner"), None),
        P(("outer", "inner"), None),
        P(("outer", "inner"), None),
        P(),
    )
    out_specs = (
        P(("outer", "inner"), None),
        P(("outer", "inner"), None),
        P(("outer", "inner"), None),
    )
    return jax.shard_map(shards, mesh=mesh, in_specs=in_specs, out_specs=out_specs, check_vma=False)
```

profile of v0, /device:TPU:6, one launch (start us, length us, event | category | flops | bytes accessed | tf_op | source)
XLA Modules:
  0.0 571.5 jit_solution(11450851049235379509)
XLA Ops:
  8.7 3.4 collective-permute-start
  12.1 2.6 collective-permute-done
  15.4 5.5 collective-permute-start.1
  20.9 1.9 collective-permute-done.1
  28.2 63.1 %all-gather.7.cloned.1.call-done = bf16[4096,128]{1,0:T(8,128)(2,1)} async-done(((bf16[128,128]{1,0:T(8,128)(2,1)}), bf16[4096,128]{1,0:T(8,128)(2,1)}) %all-gather.7.cloned.1.call-update) | async-done | bytes 1048592 | tf_op jit(solution)/shard_map/all_gather | solution.py:32
  91.2 77.2 %all-gather.11.cloned.1.call-done = bf16[4096,128]{1,0:T(8,128)(2,1)} async-done(((bf16[128,128]{1,0:T(8,128)(2,1)}), bf16[4096,128]{1,0:T(8,128)(2,1)}) %all-gather.11.cloned.1.call-update) | async-done | bytes 1048592 | tf_op jit(solution)/shard_map/all_gather | solution.py:33
  168.4 77.8 %all-gather.5.cloned.1.call-done = bf16[4096,128]{1,0:T(8,128)(2,1)} async-done(((bf16[128,128]{1,0:T(8,128)(2,1)}), bf16[4096,128]{1,0:T(8,128)(2,1)}) %all-gather.5.cloned.1.call-update) | async-done | bytes 1048592 | tf_op jit(solution)/shard_map/all_gather | solution.py:34
  246.2 77.6 %all-gather.9.cloned.1.call-done = bf16[4096,128]{1,0:T(8,128)(2,1)} async-done(((bf16[128,128]{1,0:T(8,128)(2,1)}), bf16[4096,128]{1,0:T(8,128)(2,1)}) %all-gather.9.cloned.1.call-update) | async-done | bytes 1048592 | tf_op jit(solution)/shard_map/all_gather | solution.py:35
  323.8 5.2 fusion.43
  329.1 35.2 %while.30 = (s32[]{:T(128)}, f32[1024,1]{0,1:T(1,128)S(1)}, f32[1024,1]{0,1:T(1,128)S(1)}, f32[1024,128]{1,0:T(8,128)S(1)}, s32[9,512]{1,0:T(8,128)S(1)}, /*inde...) while((s32[]{:T(128)}, f32[1024,1]{0,1:T(1,128)S(1)}, ...), condition=%wide.region_3.4_spmd.clone, body=%wide.region_0.3_spmd.clone.sunk | while | flops 410524160 | bytes 11240605 | solution.py:98
  329.9 1.6 fusion.84
  333.8 1.5 fusion.84
  337.7 1.5 fusion.84
  341.6 1.6 fusion.84
  349.5 1.5 fusion.84
  353.4 1.6 fusion.84
  357.3 1.5 fusion.84
  361.2 1.5 fusion.84
  364.7 60.3 %while.31 = (s32[]{:T(128)}, f32[1024,128]{1,0:T(8,128)S(1)}, bf16[9,512,128]{2,1,0:T(8,128)(2,1)}, bf16[9,512,128]{2,1,0:T(8,128)(2,1)}, s32[9,512]{1,0:T(8,128...) while((s32[]{:T(128)}, f32[1024,128]{1,0:T(8,128)S(1)}, ...), condition=%wide.region_6.7_spmd.clone, body=%wide.region_5.6_spmd.clone.sunk | while | flops 677119488 | bytes 12494019 | solution.py:122
  365.5 1.8 fusion.100
  372.2 1.7 fusion.100
  378.9 1.7 fusion.100
  385.6 1.7 fusion.100
  392.3 1.7 fusion.100
  399.0 1.8 fusion.100
  405.7 1.7 fusion.100
  412.4 1.8 fusion.100
  419.1 1.7 fusion.100
  427.4 2.3 pad_maximum_fusion
  429.7 124.6 %reduce-scatter.2.cloned.1.call-done = bf16[128,512]{1,0:T(8,128)(2,1)} async-done(((bf16[4096,512]{1,0:T(8,128)(2,1)}), bf16[128,512]{1,0:T(8,128)(2,1)}) %reduce-scatter.2.cloned.1.call-update) | async-done | bytes 131088 | tf_op jit(solution)/shard_map/reduce_scatter | solution.py:139
  555.2 2.9 collective-permute-start.2
  559.0 4.5 collective-permute-done.2
  (210 shorter events, 79.9 us)
Async XLA Ops:
  7.2 84.1 %all-gather.7.cloned.1.call-start = ((), (), s32[]{:S(2)}) async-start(), calls=%async_computation.2 | async-start | bytes 1081344 | tf_op jit(solution)/shard_map/all_gather | solution.py:32
  7.9 160.5 %all-gather.11.cloned.1.call-start = ((), (), s32[]{:S(2)}) async-start(), calls=%async_computation.4 | async-start | bytes 1081344 | tf_op jit(solution)/shard_map/all_gather | solution.py:33
  8.6 237.6 %all-gather.5.cloned.1.call-start = ((), (), s32[]{:S(2)}) async-start(), calls=%async_computation.1 | async-start | bytes 1081344 | tf_op jit(solution)/shard_map/all_gather | solution.py:34
  8.7 6.0 %collective-permute-start = (bf16[128,128]{1,0:T(8,128)(2,1)}, bf16[128,128]{1,0:T(8,128)(2,1)S(1)}, u32[]{:S(2)}, u32[]{:S(2)}) collective-permute-start(bf16[128,128]{1,0:T(8,128)(2,1)} %param.10), channel_id=1, source_target_pairs={{0,1},{1,2},{2,3},{3,4},{4,5},{5,6},{6,7},{8,9},{9,10},{10,11},{11... | collective-permute-start | bytes 98312 | tf_op jit(solution)/shard_map/ppermute | solution.py:10
  14.7 0.6 copy-start.2
  15.4 308.5 %all-gather.9.cloned.1.call-start = ((), (), s32[]{:S(2)}) async-start(), calls=%async_computation.3 | async-start | bytes 1081344 | tf_op jit(solution)/shard_map/all_gather | solution.py:35
  15.4 7.4 %collective-permute-start.1 = (bf16[128,128]{1,0:T(8,128)(2,1)}, bf16[128,128]{1,0:T(8,128)(2,1)S(1)}, u32[]{:S(2)}, u32[]{:S(2)}) collective-permute-start(bf16[128,128]{1,0:T(8,128)(2,1)} %param.11), channel_id=1, source_target_pairs={{0,1},{1,2},{2,3},{3,4},{4,5},{5,6},{6,7},{8,9},{9,10},{10,11},{11... | collective-permute-start | bytes 98312 | tf_op jit(solution)/shard_map/ppermute | solution.py:10
  22.8 0.6 copy-start.3
  23.4 530.9 %reduce-scatter.2.cloned.1.call-start = ((), (), s32[]{:S(2)}) async-start(), calls=%async_computation.5 | async-start | bytes 4325376 | tf_op jit(solution)/shard_map/reduce_scatter | solution.py:139
  425.0 1.3 copy-start
  425.0 1.6 copy-start.1
  555.2 8.3 %collective-permute-start.2 = (bf16[128,256]{1,0:T(8,128)(2,1)S(1)}, bf16[128,256]{1,0:T(8,128)(2,1)S(1)}, u32[]{:S(2)}, u32[]{:S(2)}) collective-permute-start(bf16[128,256]{1,0:T(8,128)(2,1)S(1)} %slice.36), channel_id=1, source_target_pairs={{1,0},{2,1},{3,2},{4,3},{5,4},{6,5},{7,6},{9,8},{10,9},{11,10},{12... | collective-permute-start | bytes 196616 | tf_op jit(solution)/shard_map/ppermute | solution.py:10
Sparse Core Ops, SparseCore 0:
  10.8 80.4 all-gather.6
  94.0 74.3 all-gather.10
  171.8 74.3 all-gather.4
  249.4 74.3 all-gather.8
  429.8 124.4 reduce-scatter.1
where the time goes:
time: 573 us; the launch traced here: 571 us
  waiting for transfers between devices  431 us (75%)
  matrix products  77.1 us (13%)
  other arithmetic  25.6 us (4%)
  between operations  13.9 us (2%)
  starting transfers between devices  12 us (2%)
  local copies, waits for them, and re-layouts  11 us (2%)
    reduce_scatter x1, waiting for transfers between devices, shards(): lax.psum_scatter(combined.astype(jnp.bfloat16), 'inner', scatter_dimensio...  125 us
    all_gather x1, waiting for transfers between devices, shards(): lax.all_gather(earlier_k, 'inner', axis=0, tiled=True)  77.8 us
    all_gather x1, waiting for transfers between devices, shards(): lax.all_gather(earlier_v, 'inner', axis=0, tiled=True)  77.6 us
    all_gather x1, waiting for transfers between devices, shards(): lax.all_gather(value_rows, 'inner', axis=0, tiled=True)  77.2 us
    all_gather x1, waiting for transfers between devices, shards(): lax.all_gather(key_rows, 'inner', axis=0, tiled=True)  63.1 us
    dot_general x9, matrix products, backward_tile(): jnp.einsum('rd,kd->rk', query_flat, key_tile, preferred_element_type=jnp....  15.7 us
    dot_general x9, matrix products, forward_tile(): jnp.einsum('rd,kd->rk', query_flat, key_tile, preferred_element_type=jnp....  13.9 us
    dot_general x9, matrix products, backward_tile(): jnp.dot(dscores, key_tile, preferred_element_type=jnp.float32)  13.5 us
  transfers between devices with their start and end apart: 8, of which 8 were waited for; matrix products, arithmetic and copies ran while one was open for 1% of the time, Pallas kernels for 0%

commit v1 on v0

--- a/solution.py
+++ b/solution.py
@@ -32,7 +32,12 @@
         lax.all_gather(key_rows, "inner", axis=0, tiled=True),
         lax.all_gather(value_rows, "inner", axis=0, tiled=True),
         lax.all_gather(earlier_k, "inner", axis=0, tiled=True),
-        lax.all_gather(earlier_v, "inner", axis=0, tiled=True),
+        jnp.concatenate(
+            lax.all_to_all(
+                jnp.stack([earlier_v for _ in range(lax.axis_size("inner"))]), "inner", 0, 0
+            ),
+            0,
+        ),
     )
     padding = jnp.zeros((pad_blocks * block_len, width), key_rows.dtype)
     keys_all = jnp.concatenate([prior_k, group_k, padding], axis=0)

time: 573 us -> 498 us (0.87)
  waiting for transfers between devices: 431 us -> 351 us
  starting transfers between devices: 12 us -> 20.9 us
    all_gather x1 -> x0, waiting for transfers between devices: 77.6 us -> none  [shards(): lax.all_gather(earlier_v, 'inner', axis=0, tiled=True)]
    all_to_all x0 -> x1, starting transfers between devices: none -> 11.2 us  [shards(): lax.all_to_all(jnp.stack([earlier_v for _ in range(lax.axis_size('inner')...]
  transfers between devices with their start and end apart: 8 -> 8, of which waited for: 8 -> 6; matrix products, arithmetic and copies ran while one was open for 1% -> 1% of each run, Pallas kernels for 0% -> 0%
where the time goes in v1:
time: 498 us; the launch traced here: 497 us
  waiting for transfers between devices  351 us (70%)
  matrix products  77 us (15%)
  other arithmetic  23.2 us (5%)
  starting transfers between devices  20.9 us (4%)
  between operations  14 us (3%)
  local copies, waits for them, and re-layouts  10 us (2%)
    reduce_scatter x1, waiting for transfers between devices, shards(): lax.psum_scatter(combined.astype(jnp.bfloat16), 'inner', scatter_dimensio...  125 us
    all_gather x1, waiting for transfers between devices, shards(): lax.all_gather(earlier_k, 'inner', axis=0, tiled=True)  77.8 us
    all_gather x1, waiting for transfers between devices, shards(): lax.all_gather(value_rows, 'inner', axis=0, tiled=True)  77.2 us
    all_gather x1, waiting for transfers between devices, shards(): lax.all_gather(key_rows, 'inner', axis=0, tiled=True)  63.1 us
    dot_general x9, matrix products, backward_tile(): jnp.einsum('rd,kd->rk', query_flat, key_tile, preferred_element_type=jnp....  15.7 us
    dot_general x9, matrix products, forward_tile(): jnp.einsum('rd,kd->rk', query_flat, key_tile, preferred_element_type=jnp....  13.9 us
    dot_general x9, matrix products, backward_tile(): jnp.dot(dscores, key_tile, preferred_element_type=jnp.float32)  13.5 us
    all_to_all x1, starting transfers between devices, shards(): lax.all_to_all(jnp.stack([earlier_v for _ in range(lax.axis_size('inner')...  11.2 us
  transfers between devices with their start and end apart: 8, of which 6 were waited for; matrix products, arithmetic and copies ran while one was open for 1% of the time, Pallas kernels for 0%

profile of v1, /device:TPU:6, one launch (start us, length us, event | category | flops | bytes accessed | tf_op | source)
XLA Modules:
  0.0 497.1 jit_solution(15244704757231253730)
XLA Ops:
  8.7 3.4 collective-permute-start
  12.1 3.4 collective-permute-start.1
  16.2 2.0 collective-permute-done.1
  19.4 11.2 %all-to-all-start = ((bf16[32,128,128]{2,1,0:T(8,128)(2,1)}), bf16[32,128,128]{2,1,0:T(8,128)(2,1)S(1)}, u32[]{:S(2)}, u32[]{:S(2)}) async-start(bf16[32,128,128]{2,1,0:T(8,128)(2,1)} %stack.2), calls=%async_computation | async-start | bytes 2097152 | tf_op jit(solution)/shard_map/all_to_all | solution.py:36
  32.0 63.1 %all-gather.6.cloned.1.call-done = bf16[4096,128]{1,0:T(8,128)(2,1)} async-done(((bf16[128,128]{1,0:T(8,128)(2,1)}), bf16[4096,128]{1,0:T(8,128)(2,1)}) %all-gather.6.cloned.1.call-update) | async-done | bytes 1048592 | tf_op jit(solution)/shard_map/all_gather | solution.py:32
  95.1 77.2 %all-gather.8.cloned.1.call-done = bf16[4096,128]{1,0:T(8,128)(2,1)} async-done(((bf16[128,128]{1,0:T(8,128)(2,1)}), bf16[4096,128]{1,0:T(8,128)(2,1)}) %all-gather.8.cloned.1.call-update) | async-done | bytes 1048592 | tf_op jit(solution)/shard_map/all_gather | solution.py:33
  172.3 77.8 %all-gather.4.cloned.1.call-done = bf16[4096,128]{1,0:T(8,128)(2,1)} async-done(((bf16[128,128]{1,0:T(8,128)(2,1)}), bf16[4096,128]{1,0:T(8,128)(2,1)}) %all-gather.4.cloned.1.call-update) | async-done | bytes 1048592 | tf_op jit(solution)/shard_map/all_gather | solution.py:34
  251.1 5.2 %fusion.43 = (bf16[4608,128]{1,0:T(8,128)(2,1)S(1)}, bf16[4608,128]{1,0:T(8,128)(2,1)}) fusion(s32[]{:T(128)S(6)} %select_n.20, bf16[4096,128]{1,0:T(8,128)(2,1)} %bitcast.126, bf16[4096,128]{1,0:T(8,128)(2,1)} %all-gather.8.cloned.1.call-done, bf16[4608]{0:T(1024)(128)(2,1)S(1)} %pad_dynamic-slice_fusion.4, ...), kind=kLoop, calls=%fused_computation.65 | loop fusion | flops 6488064 | bytes 6562820 | tf_op jit(solution)/shard_map/concatenate | solution.py:44
  256.3 34.3 %while.30 = (s32[]{:T(128)}, f32[1024,1]{0,1:T(1,128)S(1)}, f32[1024,1]{0,1:T(1,128)S(1)}, f32[1024,128]{1,0:T(8,128)S(1)}, s32[9,512]{1,0:T(8,128)S(1)}, /*inde...) while((s32[]{:T(128)}, f32[1024,1]{0,1:T(1,128)S(1)}, ...), condition=%wide.region_3.4_spmd.clone, body=%wide.region_0.3_spmd.clone.sunk | while | flops 410524160 | bytes 11240605 | solution.py:103
  257.0 1.6 fusion.84
  260.8 1.5 fusion.84
  264.6 1.5 fusion.84
  268.5 1.5 fusion.84
  272.3 1.5 fusion.84
  276.1 1.5 fusion.84
  279.9 1.5 fusion.84
  283.7 1.5 fusion.84
  287.5 1.5 fusion.84
  291.0 59.4 %while.31 = (s32[]{:T(128)}, f32[1024,128]{1,0:T(8,128)S(1)}, bf16[9,512,128]{2,1,0:T(8,128)(2,1)}, bf16[9,512,128]{2,1,0:T(8,128)(2,1)}, s32[9,512]{1,0:T(8,128...) while((s32[]{:T(128)}, f32[1024,128]{1,0:T(8,128)S(1)}, ...), condition=%wide.region_6.7_spmd.clone, body=%wide.region_5.6_spmd.clone.sunk | while | flops 677119488 | bytes 12494019 | solution.py:127
  291.7 1.7 fusion.100
  298.3 1.7 fusion.100
  304.9 1.8 fusion.100
  311.5 1.7 fusion.100
  318.1 1.7 fusion.100
  324.7 1.7 fusion.100
  331.3 1.7 fusion.100
  337.9 1.7 fusion.100
  344.5 1.7 fusion.100
  352.8 2.3 pad_maximum_fusion
  355.1 124.9 %reduce-scatter.2.cloned.1.call-done = bf16[128,512]{1,0:T(8,128)(2,1)} async-done(((bf16[4096,512]{1,0:T(8,128)(2,1)}), bf16[128,512]{1,0:T(8,128)(2,1)}) %reduce-scatter.2.cloned.1.call-update) | async-done | bytes 131088 | tf_op jit(solution)/shard_map/reduce_scatter | solution.py:144
  480.8 2.8 collective-permute-start.2
  484.5 4.6 collective-permute-done.2
  (216 shorter events, 74.8 us)
Async XLA Ops:
  7.2 23.5 %copy-start.6 = (s32[256]{0:T(256)S(1)}, s32[256]{0:T(256)}, u32[]{:S(2)}) copy-start(s32[256]{0:T(256)} %param.13) | copy-start | bytes 3076
  7.2 24.5 %copy-start.3 = (bf16[128,1024]{1,0:T(8,128)(2,1)S(1)}, bf16[128,1024]{1,0:T(8,128)(2,1)}, u32[]{:S(2)}) copy-start(bf16[128,1024]{1,0:T(8,128)(2,1)} %param.9) | copy-start | bytes 786436
  7.2 24.6 %copy-start.4 = (bf16[128,1024]{1,0:T(8,128)(2,1)S(1)}, bf16[128,1024]{1,0:T(8,128)(2,1)}, u32[]{:S(2)}) copy-start(bf16[128,1024]{1,0:T(8,128)(2,1)} %param.12) | copy-start | bytes 786436
  7.2 87.9 %all-gather.6.cloned.1.call-start = ((), (), s32[]{:S(2)}) async-start(), calls=%async_computation.3 | async-start | bytes 1081344 | tf_op jit(solution)/shard_map/all_gather | solution.py:32
  7.9 164.4 %all-gather.8.cloned.1.call-start = ((), (), s32[]{:S(2)}) async-start(), calls=%async_computation.4 | async-start | bytes 1081344 | tf_op jit(solution)/shard_map/all_gather | solution.py:33
  8.7 241.4 %all-gather.4.cloned.1.call-start = ((), (), s32[]{:S(2)}) async-start(), calls=%async_computation.2 | async-start | bytes 1081344 | tf_op jit(solution)/shard_map/all_gather | solution.py:34
  8.7 6.8 %collective-permute-start = (bf16[128,128]{1,0:T(8,128)(2,1)}, bf16[128,128]{1,0:T(8,128)(2,1)S(1)}, u32[]{:S(2)}, u32[]{:S(2)}) collective-permute-start(bf16[128,128]{1,0:T(8,128)(2,1)} %param.10), channel_id=1, source_target_pairs={{0,1},{1,2},{2,3},{3,4},{4,5},{5,6},{6,7},{8,9},{9,10},{10,11},{11... | collective-permute-start | bytes 98312 | tf_op jit(solution)/shard_map/ppermute | solution.py:10
  12.1 6.0 %collective-permute-start.1 = (bf16[128,128]{1,0:T(8,128)(2,1)}, bf16[128,128]{1,0:T(8,128)(2,1)S(1)}, u32[]{:S(2)}, u32[]{:S(2)}) collective-permute-start(bf16[128,128]{1,0:T(8,128)(2,1)} %param.11), channel_id=1, source_target_pairs={{0,1},{1,2},{2,3},{3,4},{4,5},{5,6},{6,7},{8,9},{9,10},{10,11},{11... | collective-permute-start | bytes 98312 | tf_op jit(solution)/shard_map/ppermute | solution.py:10
  15.5 0.6 copy-start.5
  19.4 230.7 %all-to-all-start = ((bf16[32,128,128]{2,1,0:T(8,128)(2,1)}), bf16[32,128,128]{2,1,0:T(8,128)(2,1)S(1)}, u32[]{:S(2)}, u32[]{:S(2)}) async-start(bf16[32,128,128]{2,1,0:T(8,128)(2,1)} %stack.2), calls=%async_computation | async-start | bytes 2097152 | tf_op jit(solution)/shard_map/all_to_all | solution.py:36
  30.6 449.4 %reduce-scatter.2.cloned.1.call-start = ((), (), s32[]{:S(2)}) async-start(), calls=%async_computation.5 | async-start | bytes 4325376 | tf_op jit(solution)/shard_map/reduce_scatter | solution.py:144
  250.1 1.0 copy-start
  350.4 1.3 copy-start.1
  350.4 1.6 copy-start.2
  480.8 8.3 %collective-permute-start.2 = (bf16[128,256]{1,0:T(8,128)(2,1)S(1)}, bf16[128,256]{1,0:T(8,128)(2,1)S(1)}, u32[]{:S(2)}, u32[]{:S(2)}) collective-permute-start(bf16[128,256]{1,0:T(8,128)(2,1)S(1)} %slice.36), channel_id=1, source_target_pairs={{1,0},{2,1},{3,2},{4,3},{5,4},{6,5},{7,6},{9,8},{10,9},{11,10},{12... | collective-permute-start | bytes 196616 | tf_op jit(solution)/shard_map/ppermute | solution.py:10
Sparse Core Ops, SparseCore 0:
  10.8 84.2 all-gather.5
  97.9 74.3 all-gather.7
  175.7 74.3 all-gather.3
  355.2 124.7 reduce-scatter.1
